TPU v7x, 512 devices: a whole 4x8x8 slice. The times are simulated.
512 devices in a mesh: loop: 16 (over x, y_lo, core), groups: 32 (over y_hi, z).
Axes of the slice: x: 4, y: 8 (y_hi: 4, y_lo: 2; y = y_hi * 2 + y_lo), z: 8, core: 2. Of those that a mesh axis runs over, the one named last changes fastest.
Arguments:
- states: bfloat16 [65536, 1024], P(('loop', 'groups')), may hold values from -64 to 64
- premises: bfloat16 [65536, 1024], P(('loop', 'groups')), may hold values from -1 to 1
- counts: int32 [16, 32], P('loop', 'groups'), may hold values from 64 to 128, as said below
- partner_mask: int32 [16], P('loop'), may hold values from 0 to 31, as said below
- send_rows: int32 [16, 32, 16], P('loop', 'groups'), may hold values from 0 to 63
- hard_idx: int32 [65536], P(('loop', 'groups')), may hold values from 0 to 15
Outputs:
- loss: float32 [], replicated
- grad_states: bfloat16 [65536, 1024], P(('loop', 'groups'))
- grad_premises: bfloat16 [65536, 1024], P(('loop', 'groups'))
Inputs may be any that keep to these rules, and one draw needn't show every extreme that they name: `counts`: at least 64 valid pairs on every device; some device has all slots valid. `partner_mask`: loop index 0 has the value 32 // 2.
All inputs are finite; a program needn't handle non-finite values.
Results may differ from a plain program's by a relative error of at most 0.0034.
Values may be sent and summed in bfloat16 or wider, within the bound.
A program may use at most 64 MiB of HBM per device.

v0:
```python
import jax
import jax.numpy as jnp
from jax import lax
from jax.sharding import PartitionSpec as P

SCALE = 3.0


def from_behind(value, axis, steps):
    count = lax.axis_size(axis)
    pairs = [(source, (source + steps) % count) for source in range(count)]
    return lax.ppermute(value, axis, pairs)


def body(states, premises, counts, partner_mask, send_rows, hard_idx):
    rows = states.shape[0]
    offer = send_rows.shape[2]
    loop_size = lax.axis_size("loop")
    group_size = lax.axis_size("groups")
    here = lax.axis_index("loop")
    group = lax.axis_index("groups")
    slots = jnp.arange(rows, dtype=jnp.int32)
    valid = slots < counts[0, 0]
    vflt = valid.astype(jnp.float32)
    partner = jnp.bitwise_xor(group, partner_mask[0])
    keys, counts_all = (
        lax.all_gather(premises, "loop", axis=0, tiled=True),
        lax.all_gather(counts, "loop", axis=0, tiled=True),
    )
    column = jnp.arange(loop_size * rows, dtype=jnp.int32)
    limits = jnp.repeat(counts_all[:, 0], rows)
    key_ok = column % rows < limits
    scores = SCALE * jnp.einsum("pd,kd->pk", states, keys, preferred_element_type=jnp.float32)
    masked = jnp.where(key_ok[None, :], scores, -jnp.inf)
    top = jnp.max(masked, axis=1)
    lse = top + jnp.log(jnp.sum(jnp.exp(masked - top[:, None]), axis=1))
    own_block = lax.dynamic_slice_in_dim(scores, here * rows, rows, 1)
    pos = jnp.diagonal(own_block)
    offered = premises[send_rows[0, 0]]
    piece = lax.all_gather(offered, "groups", axis=0, tiled=True)
    offset = partner * offer
    count = piece.shape[0]
    inside = jnp.logical_and(offset >= 0, offset < count)
    part = lax.dynamic_slice_in_dim(piece, jnp.clip(offset, 0, count - offer), offer, 0)
    pool = jnp.where(inside, part, jnp.zeros_like(offered))
    hard = pool[hard_idx]
    states_f = states.astype(jnp.float32)
    hard_f = hard.astype(jnp.float32)
    tval = SCALE * jnp.sum(states_f * hard_f, axis=-1)
    qval = jnp.where(valid, jax.nn.sigmoid(tval - pos), 0.0)
    terms = jnp.where(valid, lse - pos + jax.nn.softplus(tval - pos), 0.0)
    loss = lax.psum(jnp.sum(terms), ("loop", "groups")) / (loop_size * group_size * rows)
    prob = jnp.where(valid[:, None], jnp.exp(masked - lse[:, None]), 0.0).astype(jnp.bfloat16)
    dstate = jnp.dot(prob, keys, preferred_element_type=jnp.float32)
    grad_states = SCALE * (
        dstate + qval[:, None] * hard_f - (vflt + qval)[:, None] * premises.astype(jnp.float32)
    )

    def visit(step, carry):
        block = jnp.remainder(here - step, loop_size)
        columns = lax.dynamic_slice_in_dim(prob, block * rows, rows, 1)
        carry = carry + jnp.einsum("pk,pd->kd", columns, states, preferred_element_type=jnp.float32)
        return from_behind(carry.astype(jnp.bfloat16), "loop", 1).astype(carry.dtype)

    dprem = lax.fori_loop(0, loop_size, visit, jnp.zeros(states.shape, jnp.float32))
    pick = jax.nn.one_hot(hard_idx, offer, dtype=jnp.float32)
    back = SCALE * jnp.dot(pick.T, qval[:, None] * states_f, precision=lax.Precision.HIGHEST)
    piece = lax.all_gather(back, "groups", axis=0, tiled=True)
    offset = partner * offer
    count = piece.shape[0]
    inside = jnp.logical_and(offset >= 0, offset < count)
    part = lax.dynamic_slice_in_dim(piece, jnp.clip(offset, 0, count - offer), offer, 0)
    back_home = jnp.where(inside, part, jnp.zeros_like(back))
    place = jax.nn.one_hot(send_rows[0, 0], rows, dtype=jnp.float32)
    dhard = jnp.dot(place.T, back_home, precision=lax.Precision.HIGHEST)
    grad_premises = dprem - SCALE * (vflt + qval)[:, None] * states_f + dhard
    return (loss, grad_states.astype(jnp.bfloat16), grad_premises.astype(jnp.bfloat16))


def solution(mesh):
    return jax.shard_map(
        body,
        mesh=mesh,
        in_specs=(
            P(("loop", "groups"), None),
            P(("loop", "groups"), None),
            P("loop", "groups"),
            P("loop"),
            P("loop", "groups", None),
            P(("loop", "groups")),
        ),
        out_specs=(P(), P(("loop", "groups"), None), P(("loop", "groups"), None)),
        check_vma=False,
    )
```

profile of v0, /device:TPU:16, one launch (start us, length us, event | category | flops | bytes accessed | tf_op | source)
XLA Modules:
  0.0 425.0 jit_solution(1148805048968045579)
XLA Ops:
  7.9 2.2 gather_fusion.1
  14.2 12.4 %all-reduce = s32[16]{0:T(128)S(1)} all-reduce(s32[16]{0:T(128)S(1)} %bitcast_dynamic-update-slice_fusion), channel_id=1, replica_groups=mesh['loop'=16,'groups'=32] {'loop'}, use_global_device_ids=true, to_apply=%add | all-reduce | flops 16 | bytes 128
  27.4 71.7 %all-gather.9.cloned.1.call-done = bf16[512,1024]{1,0:T(8,128)(2,1)} async-done(((bf16[16,1024]{1,0:T(8,128)(2,1)}), bf16[512,1024]{1,0:T(8,128)(2,1)}) %all-gather.9.cloned.1.call-update) | async-done | bytes 1048592 | tf_op jit(solution)/shard_map/all_gather | solution.py:40
  102.0 38.2 %all-gather.5.cloned.1.call-done = bf16[2048,1024]{1,0:T(8,128)(2,1)} async-done(((bf16[128,1024]{1,0:T(8,128)(2,1)}), bf16[2048,1024]{1,0:T(8,128)(2,1)}) %all-gather.5.cloned.1.call-update) | async-done | bytes 4194320 | tf_op jit(solution)/shard_map/all_gather | solution.py:27
  140.1 3.9 select_reduce_fusion
  147.7 3.7 fusion.5
  151.4 100.6 %psum.7 = f32[]{:T(128)} all-reduce(f32[]{:T(128)} %get-tuple-element.170), channel_id=1, replica_groups=mesh['loop'=16,'groups'=32] {'loop','groups'}, use_global_device_ids=true, to_apply=%region_4.5 | all-reduce | flops 1 | bytes 8 | tf_op jit(solution)/shard_map/psum | solution.py:52
  252.7 162.5 %while.16 = (s32[]{:T(128)}, f32[128,1024]{1,0:T(8,128)S(1)}, s32[]{:T(128)}, bf16[128,2048]{1,0:T(8,128)(2,1)S(1)}, bf16[128,1024]{1,0:T(8,128)(2,1)S(1)}, /*in...) while((s32[]{:T(128)}, f32[128,1024]{1,0:T(8,128)S(1)}, ...), condition=%wide.region_6.7_spmd.clone, body=%wide.region_5.6_spmd.clone.sunk | while | flops 34078736 | bytes 2916682 | solution.py:65
  253.0 1.9 collective-permute-start
  254.9 7.9 %collective-permute-done = bf16[128,1024]{1,0:T(8,128)(2,1)S(1)} collective-permute-done((bf16[128,1024]{1,0:T(8,128)(2,1)S(1)}, bf16[128,1024]{1,0:T(8,128)(2,1)S(1)}, u32[]{:S(2)}, u32[]{:S(2)}) %collective-permute-start) | collective-permute-done | bytes 262176 | tf_op jit(solution)/shard_map/while/body/eval_jaxpr/ppermute | solution.py:12
  263.1 1.9 collective-permute-start
  265.0 7.9 %collective-permute-done = bf16[128,1024]{1,0:T(8,128)(2,1)S(1)} collective-permute-done((bf16[128,1024]{1,0:T(8,128)(2,1)S(1)}, bf16[128,1024]{1,0:T(8,128)(2,1)S(1)}, u32[]{:S(2)}, u32[]{:S(2)}) %collective-permute-start) | collective-permute-done | bytes 262176 | tf_op jit(solution)/shard_map/while/body/eval_jaxpr/ppermute | solution.py:12
  273.3 1.9 collective-permute-start
  275.2 7.9 %collective-permute-done = bf16[128,1024]{1,0:T(8,128)(2,1)S(1)} collective-permute-done((bf16[128,1024]{1,0:T(8,128)(2,1)S(1)}, bf16[128,1024]{1,0:T(8,128)(2,1)S(1)}, u32[]{:S(2)}, u32[]{:S(2)}) %collective-permute-start) | collective-permute-done | bytes 262176 | tf_op jit(solution)/shard_map/while/body/eval_jaxpr/ppermute | solution.py:12
  283.4 1.9 collective-permute-start
  285.3 7.9 %collective-permute-done = bf16[128,1024]{1,0:T(8,128)(2,1)S(1)} collective-permute-done((bf16[128,1024]{1,0:T(8,128)(2,1)S(1)}, bf16[128,1024]{1,0:T(8,128)(2,1)S(1)}, u32[]{:S(2)}, u32[]{:S(2)}) %collective-permute-start) | collective-permute-done | bytes 262176 | tf_op jit(solution)/shard_map/while/body/eval_jaxpr/ppermute | solution.py:12
  293.6 1.9 collective-permute-start
  295.5 7.9 %collective-permute-done = bf16[128,1024]{1,0:T(8,128)(2,1)S(1)} collective-permute-done((bf16[128,1024]{1,0:T(8,128)(2,1)S(1)}, bf16[128,1024]{1,0:T(8,128)(2,1)S(1)}, u32[]{:S(2)}, u32[]{:S(2)}) %collective-permute-start) | collective-permute-done | bytes 262176 | tf_op jit(solution)/shard_map/while/body/eval_jaxpr/ppermute | solution.py:12
  305.7 7.9 %collective-permute-done = bf16[128,1024]{1,0:T(8,128)(2,1)S(1)} collective-permute-done((bf16[128,1024]{1,0:T(8,128)(2,1)S(1)}, bf16[128,1024]{1,0:T(8,128)(2,1)S(1)}, u32[]{:S(2)}, u32[]{:S(2)}) %collective-permute-start) | collective-permute-done | bytes 262176 | tf_op jit(solution)/shard_map/while/body/eval_jaxpr/ppermute | solution.py:12
  315.8 7.9 %collective-permute-done = bf16[128,1024]{1,0:T(8,128)(2,1)S(1)} collective-permute-done((bf16[128,1024]{1,0:T(8,128)(2,1)S(1)}, bf16[128,1024]{1,0:T(8,128)(2,1)S(1)}, u32[]{:S(2)}, u32[]{:S(2)}) %collective-permute-start) | collective-permute-done | bytes 262176 | tf_op jit(solution)/shard_map/while/body/eval_jaxpr/ppermute | solution.py:12
  326.0 7.9 %collective-permute-done = bf16[128,1024]{1,0:T(8,128)(2,1)S(1)} collective-permute-done((bf16[128,1024]{1,0:T(8,128)(2,1)S(1)}, bf16[128,1024]{1,0:T(8,128)(2,1)S(1)}, u32[]{:S(2)}, u32[]{:S(2)}) %collective-permute-start) | collective-permute-done | bytes 262176 | tf_op jit(solution)/shard_map/while/body/eval_jaxpr/ppermute | solution.py:12
  336.1 7.9 %collective-permute-done = bf16[128,1024]{1,0:T(8,128)(2,1)S(1)} collective-permute-done((bf16[128,1024]{1,0:T(8,128)(2,1)S(1)}, bf16[128,1024]{1,0:T(8,128)(2,1)S(1)}, u32[]{:S(2)}, u32[]{:S(2)}) %collective-permute-start) | collective-permute-done | bytes 262176 | tf_op jit(solution)/shard_map/while/body/eval_jaxpr/ppermute | solution.py:12
  346.3 7.9 %collective-permute-done = bf16[128,1024]{1,0:T(8,128)(2,1)S(1)} collective-permute-done((bf16[128,1024]{1,0:T(8,128)(2,1)S(1)}, bf16[128,1024]{1,0:T(8,128)(2,1)S(1)}, u32[]{:S(2)}, u32[]{:S(2)}) %collective-permute-start) | collective-permute-done | bytes 262176 | tf_op jit(solution)/shard_map/while/body/eval_jaxpr/ppermute | solution.py:12
  356.4 7.9 %collective-permute-done = bf16[128,1024]{1,0:T(8,128)(2,1)S(1)} collective-permute-done((bf16[128,1024]{1,0:T(8,128)(2,1)S(1)}, bf16[128,1024]{1,0:T(8,128)(2,1)S(1)}, u32[]{:S(2)}, u32[]{:S(2)}) %collective-permute-start) | collective-permute-done | bytes 262176 | tf_op jit(solution)/shard_map/while/body/eval_jaxpr/ppermute | solution.py:12
  366.6 7.9 %collective-permute-done = bf16[128,1024]{1,0:T(8,128)(2,1)S(1)} collective-permute-done((bf16[128,1024]{1,0:T(8,128)(2,1)S(1)}, bf16[128,1024]{1,0:T(8,128)(2,1)S(1)}, u32[]{:S(2)}, u32[]{:S(2)}) %collective-permute-start) | collective-permute-done | bytes 262176 | tf_op jit(solution)/shard_map/while/body/eval_jaxpr/ppermute | solution.py:12
  376.7 7.9 %collective-permute-done = bf16[128,1024]{1,0:T(8,128)(2,1)S(1)} collective-permute-done((bf16[128,1024]{1,0:T(8,128)(2,1)S(1)}, bf16[128,1024]{1,0:T(8,128)(2,1)S(1)}, u32[]{:S(2)}, u32[]{:S(2)}) %collective-permute-start) | collective-permute-done | bytes 262176 | tf_op jit(solution)/shard_map/while/body/eval_jaxpr/ppermute | solution.py:12
  385.0 1.9 collective-permute-start
  386.9 7.9 %collective-permute-done = bf16[128,1024]{1,0:T(8,128)(2,1)S(1)} collective-permute-done((bf16[128,1024]{1,0:T(8,128)(2,1)S(1)}, bf16[128,1024]{1,0:T(8,128)(2,1)S(1)}, u32[]{:S(2)}, u32[]{:S(2)}) %collective-permute-start) | collective-permute-done | bytes 262176 | tf_op jit(solution)/shard_map/while/body/eval_jaxpr/ppermute | solution.py:12
  397.1 7.9 %collective-permute-done = bf16[128,1024]{1,0:T(8,128)(2,1)S(1)} collective-permute-done((bf16[128,1024]{1,0:T(8,128)(2,1)S(1)}, bf16[128,1024]{1,0:T(8,128)(2,1)S(1)}, u32[]{:S(2)}, u32[]{:S(2)}) %collective-permute-start) | collective-permute-done | bytes 262176 | tf_op jit(solution)/shard_map/while/body/eval_jaxpr/ppermute | solution.py:12
  405.3 1.9 collective-permute-start
  407.2 7.9 %collective-permute-done = bf16[128,1024]{1,0:T(8,128)(2,1)S(1)} collective-permute-done((bf16[128,1024]{1,0:T(8,128)(2,1)S(1)}, bf16[128,1024]{1,0:T(8,128)(2,1)S(1)}, u32[]{:S(2)}, u32[]{:S(2)}) %collective-permute-start) | collective-permute-done | bytes 262176 | tf_op jit(solution)/shard_map/while/body/eval_jaxpr/ppermute | solution.py:12
  415.2 2.1 fusion.6
  (76 shorter events, 32.8 us)
Async XLA Ops:
  7.2 91.9 %all-gather.9.cloned.1.call-start = ((), (), s32[]{:S(2)}) async-start(), calls=%async_computation.2 | async-start | bytes 1081344 | tf_op jit(solution)/shard_map/all_gather | solution.py:40
  10.1 130.0 %all-gather.5.cloned.1.call-start = ((), (), s32[]{:S(2)}) async-start(), calls=%async_computation | async-start | bytes 4456448 | tf_op jit(solution)/shard_map/all_gather | solution.py:27
  10.9 404.3 %all-gather.7.cloned.1.call-start = ((), (), s32[]{:S(2)}) async-start(), calls=%async_computation.1 | async-start | bytes 2162688 | tf_op jit(solution)/shard_map/all_gather | solution.py:68
  100.8 45.5 %copy-start = (bf16[128,1024]{1,0:T(8,128)(2,1)S(1)}, bf16[128,1024]{1,0:T(8,128)(2,1)}, u32[]{:S(2)}) copy-start(bf16[128,1024]{1,0:T(8,128)(2,1)} %param.8) | copy-start | bytes 786436
  100.8 45.5 %copy-start.2 = (s32[128]{0:T(128)S(1)}, s32[128]{0:T(128)}, u32[]{:S(2)}) copy-start(s32[128]{0:T(128)} %param.13) | copy-start | bytes 1540
  102.0 45.7 %copy-start.1 = (bf16[128,1024]{1,0:T(8,128)(2,1)S(1)}, bf16[128,1024]{1,0:T(8,128)(2,1)}, u32[]{:S(2)}) copy-start(bf16[128,1024]{1,0:T(8,128)(2,1)} %param.9) | copy-start | bytes 786436
  252.6 162.5 %copy-start.3 = (s32[1,1,16]{2,1,0:T(1,128)S(1)}, s32[1,1,16]{2,1,0:T(1,128)}, u32[]{:S(2)}) copy-start(s32[1,1,16]{2,1,0:T(1,128)} %param.12) | copy-start | bytes 196
  253.0 9.8 %collective-permute-start = (bf16[128,1024]{1,0:T(8,128)(2,1)S(1)}, bf16[128,1024]{1,0:T(8,128)(2,1)S(1)}, u32[]{:S(2)}, u32[]{:S(2)}) collective-permute-start(bf16[128,1024]{1,0:T(8,128)(2,1)S(1)} %fusion.36), channel_id=1, source_target_pairs={{0,32},{32,64},{64,96},{96,128},{128,160},{160,192},{192,224},{224... | collective-permute-start | bytes 786440 | tf_op jit(solution)/shard_map/while/body/eval_jaxpr/ppermute | solution.py:12
  263.1 9.8 %collective-permute-start = (bf16[128,1024]{1,0:T(8,128)(2,1)S(1)}, bf16[128,1024]{1,0:T(8,128)(2,1)S(1)}, u32[]{:S(2)}, u32[]{:S(2)}) collective-permute-start(bf16[128,1024]{1,0:T(8,128)(2,1)S(1)} %fusion.36), channel_id=1, source_target_pairs={{0,32},{32,64},{64,96},{96,128},{128,160},{160,192},{192,224},{224... | collective-permute-start | bytes 786440 | tf_op jit(solution)/shard_map/while/body/eval_jaxpr/ppermute | solution.py:12
  273.3 9.8 %collective-permute-start = (bf16[128,1024]{1,0:T(8,128)(2,1)S(1)}, bf16[128,1024]{1,0:T(8,128)(2,1)S(1)}, u32[]{:S(2)}, u32[]{:S(2)}) collective-permute-start(bf16[128,1024]{1,0:T(8,128)(2,1)S(1)} %fusion.36), channel_id=1, source_target_pairs={{0,32},{32,64},{64,96},{96,128},{128,160},{160,192},{192,224},{224... | collective-permute-start | bytes 786440 | tf_op jit(solution)/shard_map/while/body/eval_jaxpr/ppermute | solution.py:12
  283.4 9.8 %collective-permute-start = (bf16[128,1024]{1,0:T(8,128)(2,1)S(1)}, bf16[128,1024]{1,0:T(8,128)(2,1)S(1)}, u32[]{:S(2)}, u32[]{:S(2)}) collective-permute-start(bf16[128,1024]{1,0:T(8,128)(2,1)S(1)} %fusion.36), channel_id=1, source_target_pairs={{0,32},{32,64},{64,96},{96,128},{128,160},{160,192},{192,224},{224... | collective-permute-start | bytes 786440 | tf_op jit(solution)/shard_map/while/body/eval_jaxpr/ppermute | solution.py:12
  293.6 9.8 %collective-permute-start = (bf16[128,1024]{1,0:T(8,128)(2,1)S(1)}, bf16[128,1024]{1,0:T(8,128)(2,1)S(1)}, u32[]{:S(2)}, u32[]{:S(2)}) collective-permute-start(bf16[128,1024]{1,0:T(8,128)(2,1)S(1)} %fusion.36), channel_id=1, source_target_pairs={{0,32},{32,64},{64,96},{96,128},{128,160},{160,192},{192,224},{224... | collective-permute-start | bytes 786440 | tf_op jit(solution)/shard_map/while/body/eval_jaxpr/ppermute | solution.py:12
  303.7 9.8 %collective-permute-start = (bf16[128,1024]{1,0:T(8,128)(2,1)S(1)}, bf16[128,1024]{1,0:T(8,128)(2,1)S(1)}, u32[]{:S(2)}, u32[]{:S(2)}) collective-permute-start(bf16[128,1024]{1,0:T(8,128)(2,1)S(1)} %fusion.36), channel_id=1, source_target_pairs={{0,32},{32,64},{64,96},{96,128},{128,160},{160,192},{192,224},{224... | collective-permute-start | bytes 786440 | tf_op jit(solution)/shard_map/while/body/eval_jaxpr/ppermute | solution.py:12
  313.9 9.8 %collective-permute-start = (bf16[128,1024]{1,0:T(8,128)(2,1)S(1)}, bf16[128,1024]{1,0:T(8,128)(2,1)S(1)}, u32[]{:S(2)}, u32[]{:S(2)}) collective-permute-start(bf16[128,1024]{1,0:T(8,128)(2,1)S(1)} %fusion.36), channel_id=1, source_target_pairs={{0,32},{32,64},{64,96},{96,128},{128,160},{160,192},{192,224},{224... | collective-permute-start | bytes 786440 | tf_op jit(solution)/shard_map/while/body/eval_jaxpr/ppermute | solution.py:12
  324.0 9.8 %collective-permute-start = (bf16[128,1024]{1,0:T(8,128)(2,1)S(1)}, bf16[128,1024]{1,0:T(8,128)(2,1)S(1)}, u32[]{:S(2)}, u32[]{:S(2)}) collective-permute-start(bf16[128,1024]{1,0:T(8,128)(2,1)S(1)} %fusion.36), channel_id=1, source_target_pairs={{0,32},{32,64},{64,96},{96,128},{128,160},{160,192},{192,224},{224... | collective-permute-start | bytes 786440 | tf_op jit(solution)/shard_map/while/body/eval_jaxpr/ppermute | solution.py:12
  334.2 9.8 %collective-permute-start = (bf16[128,1024]{1,0:T(8,128)(2,1)S(1)}, bf16[128,1024]{1,0:T(8,128)(2,1)S(1)}, u32[]{:S(2)}, u32[]{:S(2)}) collective-permute-start(bf16[128,1024]{1,0:T(8,128)(2,1)S(1)} %fusion.36), channel_id=1, source_target_pairs={{0,32},{32,64},{64,96},{96,128},{128,160},{160,192},{192,224},{224... | collective-permute-start | bytes 786440 | tf_op jit(solution)/shard_map/while/body/eval_jaxpr/ppermute | solution.py:12
  344.4 9.8 %collective-permute-start = (bf16[128,1024]{1,0:T(8,128)(2,1)S(1)}, bf16[128,1024]{1,0:T(8,128)(2,1)S(1)}, u32[]{:S(2)}, u32[]{:S(2)}) collective-permute-start(bf16[128,1024]{1,0:T(8,128)(2,1)S(1)} %fusion.36), channel_id=1, source_target_pairs={{0,32},{32,64},{64,96},{96,128},{128,160},{160,192},{192,224},{224... | collective-permute-start | bytes 786440 | tf_op jit(solution)/shard_map/while/body/eval_jaxpr/ppermute | solution.py:12
  354.5 9.8 %collective-permute-start = (bf16[128,1024]{1,0:T(8,128)(2,1)S(1)}, bf16[128,1024]{1,0:T(8,128)(2,1)S(1)}, u32[]{:S(2)}, u32[]{:S(2)}) collective-permute-start(bf16[128,1024]{1,0:T(8,128)(2,1)S(1)} %fusion.36), channel_id=1, source_target_pairs={{0,32},{32,64},{64,96},{96,128},{128,160},{160,192},{192,224},{224... | collective-permute-start | bytes 786440 | tf_op jit(solution)/shard_map/while/body/eval_jaxpr/ppermute | solution.py:12
  364.7 9.8 %collective-permute-start = (bf16[128,1024]{1,0:T(8,128)(2,1)S(1)}, bf16[128,1024]{1,0:T(8,128)(2,1)S(1)}, u32[]{:S(2)}, u32[]{:S(2)}) collective-permute-start(bf16[128,1024]{1,0:T(8,128)(2,1)S(1)} %fusion.36), channel_id=1, source_target_pairs={{0,32},{32,64},{64,96},{96,128},{128,160},{160,192},{192,224},{224... | collective-permute-start | bytes 786440 | tf_op jit(solution)/shard_map/while/body/eval_jaxpr/ppermute | solution.py:12
  374.8 9.8 %collective-permute-start = (bf16[128,1024]{1,0:T(8,128)(2,1)S(1)}, bf16[128,1024]{1,0:T(8,128)(2,1)S(1)}, u32[]{:S(2)}, u32[]{:S(2)}) collective-permute-start(bf16[128,1024]{1,0:T(8,128)(2,1)S(1)} %fusion.36), channel_id=1, source_target_pairs={{0,32},{32,64},{64,96},{96,128},{128,160},{160,192},{192,224},{224... | collective-permute-start | bytes 786440 | tf_op jit(solution)/shard_map/while/body/eval_jaxpr/ppermute | solution.py:12
  385.0 9.8 %collective-permute-start = (bf16[128,1024]{1,0:T(8,128)(2,1)S(1)}, bf16[128,1024]{1,0:T(8,128)(2,1)S(1)}, u32[]{:S(2)}, u32[]{:S(2)}) collective-permute-start(bf16[128,1024]{1,0:T(8,128)(2,1)S(1)} %fusion.36), channel_id=1, source_target_pairs={{0,32},{32,64},{64,96},{96,128},{128,160},{160,192},{192,224},{224... | collective-permute-start | bytes 786440 | tf_op jit(solution)/shard_map/while/body/eval_jaxpr/ppermute | solution.py:12
  395.1 9.8 %collective-permute-start = (bf16[128,1024]{1,0:T(8,128)(2,1)S(1)}, bf16[128,1024]{1,0:T(8,128)(2,1)S(1)}, u32[]{:S(2)}, u32[]{:S(2)}) collective-permute-start(bf16[128,1024]{1,0:T(8,128)(2,1)S(1)} %fusion.36), channel_id=1, source_target_pairs={{0,32},{32,64},{64,96},{96,128},{128,160},{160,192},{192,224},{224... | collective-permute-start | bytes 786440 | tf_op jit(solution)/shard_map/while/body/eval_jaxpr/ppermute | solution.py:12
  405.3 9.8 %collective-permute-start = (bf16[128,1024]{1,0:T(8,128)(2,1)S(1)}, bf16[128,1024]{1,0:T(8,128)(2,1)S(1)}, u32[]{:S(2)}, u32[]{:S(2)}) collective-permute-start(bf16[128,1024]{1,0:T(8,128)(2,1)S(1)} %fusion.36), channel_id=1, source_target_pairs={{0,32},{32,64},{64,96},{96,128},{128,160},{160,192},{192,224},{224... | collective-permute-start | bytes 786440 | tf_op jit(solution)/shard_map/while/body/eval_jaxpr/ppermute | solution.py:12
Sparse Core Ops, SparseCore 0:
  11.7 87.3 all-gather.8
  101.2 38.8 all-gather.4
  147.5 86.5 all-gather.6
where the time goes:
time: 426 us; the launch traced here: 425 us
  waiting for transfers between devices  237 us (56%)
  blocking collectives  113 us (27%)
  starting transfers between devices  30.8 us (7%)
  between operations  17 us (4%)
  matrix products  14.9 us (3%)
  local copies, waits for them, and re-layouts  6.3 us (1%)
  other arithmetic  5.34 us (1%)
    ppermute x16, waiting for transfers between devices, from_behind(): return lax.ppermute(value, axis, pairs)  126 us
    psum x1, blocking collectives, body(): lax.psum(jnp.sum(terms), ('loop', 'groups'))  101 us
    all_gather x1, waiting for transfers between devices, body(): piece = lax.all_gather(offered, 'groups', axis=0, tiled=True)  71.7 us
    all_gather x1, waiting for transfers between devices, body(): lax.all_gather(premises, 'loop', axis=0, tiled=True)  38.2 us
    ppermute x16, starting transfers between devices, from_behind(): return lax.ppermute(value, axis, pairs)  30.7 us
    unnamed x1, blocking collectives  12.4 us
  transfers between devices with their start and end apart: 19, of which 18 were waited for; matrix products, arithmetic and copies ran while one was open for 3% of the time, Pallas kernels for 0%

commit v1 on v0

v1 whole, which is shorter than its diff:
```python
import functools

import jax
import jax.numpy as jnp
from jax import lax
from jax.experimental import pallas as pl
from jax.experimental.pallas import tpu as pltpu
from jax.sharding import PartitionSpec as P

SCALE = 3.0
NX, NC, NZ, NY = 4, 4, 8, 4
F32 = jnp.float32
BF16 = jnp.bfloat16
NN = (((1,), (0,)), ((), ()))
NT = (((1,), (1,)), ((), ()))
TN = (((0,), (0,)), ((), ()))


def dot(a, b, dims, precision=None):
    return lax.dot_general(a, b, dims, preferred_element_type=F32, precision=precision)


def kernel(
    counts_ref, mask_ref, send_ref, hidx_ref, states_hbm, prem_hbm,
    loss_ref, gs_hbm, gp_hbm,
    sall, pall, cntx, cnty, zbuf, ybuf, byuf, bzuf,
    ebuf, ptbuf, stats, hardb, own_s, own_p,
    dsend, r1, rx, psend, rp, lossx, lossc, lossy, lossz, gsb, gpb,
    local_sem, xs, xr, ys, yr, cs, cr, zs, zr, ts, tr, rs, rr, ps, pr, ls, lr,
):
    rows, width = states_hbm.shape
    half = rows // 2
    offer = zbuf.shape[1]
    me = lax.axis_index("loop")
    g = lax.axis_index("groups")
    x, yc = me // NC, me % NC
    yh, z = g // NZ, g % NZ
    top, bot = pl.ds(0, half), pl.ds(half, half)

    def xdev(step):
        return {"loop": ((x + step) % NX) * NC + yc, "groups": g}

    def cdev(flip):
        y, c = yc // 2, yc % 2
        y = (y + flip // 2) % 2
        c = (c + flip % 2) % 2
        return {"loop": x * NC + y * 2 + c, "groups": g}

    def zdev(step):
        return {"loop": me, "groups": yh * NZ + (z + step) % NZ}

    def ydev(step):
        return {"loop": me, "groups": ((yh + step) % NY) * NZ + z}

    sent = []

    def send(src, dst, ssem, rsem, device):
        copy = pltpu.make_async_remote_copy(
            src_ref=src, dst_ref=dst, send_sem=ssem, recv_sem=rsem,
            device_id=device, device_id_type=pl.DeviceIdType.MESH,
        )
        copy.start()
        sent.append(copy)
        return copy

    def spread(buf, n, devs, ssem, rsem, base=0):
        return [
            send(buf.at[0], buf.at[n - i], ssem.at[base + i], rsem.at[base + n - i], devs(i))
            for i in range(1, n)
        ]

    def spread_xor(buf, ssem, rsem, base=0):
        return [
            send(buf.at[0], buf.at[i], ssem.at[base + i], rsem.at[base + i], cdev(i))
            for i in range(1, NC)
        ]

    def arrive(copies):
        for copy in copies:
            copy.wait_recv()

    load_p = pltpu.make_async_copy(prem_hbm, pall.at[0], local_sem.at[0])
    load_s = pltpu.make_async_copy(states_hbm, sall.at[0], local_sem.at[1])
    load_p.start()
    load_s.start()

    barrier = pltpu.get_barrier_semaphore()
    peers = [xdev(i) for i in range(1, NX)] + [cdev(i) for i in range(1, NC)]
    peers += [zdev(i) for i in range(1, NZ)] + [ydev(i) for i in range(1, NY)]
    for peer in peers:
        pl.semaphore_signal(barrier, inc=1, device_id=peer, device_id_type=pl.DeviceIdType.MESH)

    count = counts_ref[0, 0]
    mask = mask_ref[0]
    cntx[0] = jnp.full(cntx.shape[1:], count, jnp.int32)
    cnty[0] = jnp.full(cnty.shape[1:], count, jnp.int32)
    place = lax.broadcasted_iota(jnp.int32, (rows, offer), 0) == send_ref[...]
    place = place.astype(F32).astype(BF16)
    load_p.wait()
    zbuf[0] = dot(place, pall[0], TN).astype(BF16)
    load_s.wait()
    pl.semaphore_wait(barrier, len(peers))

    offers_z = spread(zbuf, NZ, zdev, zs, zr)
    right_a = send(sall.at[0, top], sall.at[3, top], xs.at[0], xr.at[0], xdev(1))
    left_a = send(sall.at[0, bot], sall.at[1, bot], xs.at[1], xr.at[1], xdev(3))
    over_a = send(pall.at[0, top], pall.at[2, top], ys.at[0], yr.at[0], cdev(2))
    over_b = send(pall.at[0, bot], pall.at[2, bot], ys.at[1], yr.at[1], cdev(2))
    right_b = send(sall.at[0, bot], sall.at[3, bot], xs.at[2], xr.at[2], xdev(1))
    left_b = send(sall.at[0, top], sall.at[1, top], xs.at[3], xr.at[3], xdev(3))
    twin = send(pall.at[0], pall.at[1], ys.at[2], yr.at[2], cdev(1))
    counts_x = spread(cntx, NX, xdev, cs, cr)
    counts_c = spread_xor(cnty, cs, cr, NX)

    states_f = sall[0].astype(F32)
    prem_f = pall[0].astype(F32)
    pos = SCALE * jnp.sum(states_f * prem_f, axis=1, keepdims=True)
    valid = lax.broadcasted_iota(jnp.int32, (rows, 1), 0) < count
    vflt = valid.astype(F32)

    right_a.wait_recv()
    fwd_r = send(sall.at[3, top], sall.at[2, top], xs.at[4], xr.at[4], xdev(1))
    left_a.wait_recv()
    fwd_l = send(sall.at[1, bot], sall.at[2, bot], xs.at[5], xr.at[5], xdev(3))
    over_a.wait_recv()
    twin_a = send(pall.at[2, top], pall.at[3, top], ys.at[3], yr.at[3], cdev(1))
    over_b.wait_recv()
    twin_b = send(pall.at[2, bot], pall.at[3, bot], ys.at[4], yr.at[4], cdev(1))

    mz, my = mask % NZ, mask // NZ
    pick_z = ((z ^ mz) + NZ - z) % NZ
    pick_y = ((yh ^ my) + NY - yh) % NY

    arrive(offers_z)
    ybuf[0] = zbuf[pick_z]
    offers_y = spread(ybuf, NY, ydev, zs, zr, NZ)

    arrive([right_b, left_b, twin, twin_a, twin_b] + counts_x + counts_c)
    key = lax.broadcasted_iota(jnp.int32, (rows, rows), 0)
    keys_ok = [key < cnty[b, 0:1] for b in range(NC)]
    row = lax.broadcasted_iota(jnp.int32, (1, rows), 1)

    def scores(a):
        block = SCALE * dot(pall[...].reshape(NC * rows, width), sall[a], NT)
        parts = [
            jnp.where(keys_ok[b], block[b * rows:(b + 1) * rows], -jnp.inf) for b in range(NC)
        ]
        tops = [jnp.max(part, axis=0, keepdims=True) for part in parts]
        best = jnp.maximum(jnp.maximum(tops[0], tops[1]), jnp.maximum(tops[2], tops[3]))
        total = jnp.zeros((1, rows), F32)
        for b, part in enumerate(parts):
            part = jnp.exp(part - best)
            total = total + jnp.sum(part, axis=0, keepdims=True)
            ebuf[b * rows:(b + 1) * rows, a * rows:(a + 1) * rows] = part
        stats[0, a:a + 1] = best
        stats[0, NX + a:NX + a + 1] = total

    for a in (0, 1, 3):
        scores(a)
    arrive([fwd_r, fwd_l])
    scores(2)
    stats_x = spread(stats, NX, xdev, ts, tr)

    arrive(offers_y)
    pool = ybuf[pick_y]
    pick = lax.broadcasted_iota(jnp.int32, (offer, rows), 0) == hidx_ref[...]
    pick = pick.astype(F32)
    hard = dot(pick.astype(BF16), pool, TN)
    hardb[...] = hard.astype(BF16)
    states_f = sall[0].astype(F32)
    tval = SCALE * jnp.sum(states_f * hard, axis=1, keepdims=True)
    gap = tval - pos
    soft = jnp.maximum(gap, 0.0) + jnp.log1p(jnp.exp(-jnp.abs(gap)))
    qval = jnp.where(valid, jax.nn.sigmoid(gap), 0.0)
    back = SCALE * dot(pick, qval * states_f, NN, lax.Precision.HIGHEST)
    byuf[0] = back.astype(BF16)
    back_y = spread(byuf, NY, ydev, ts, tr, NX)

    arrive(stats_x)
    own_lse = None
    for a in range(NX):
        best = [stats[d, (a + NX - d) % NX:(a + NX - d) % NX + 1] for d in range(NX)]
        part = [stats[d, NX + (a + NX - d) % NX:NX + (a + NX - d) % NX + 1] for d in range(NX)]
        high = jnp.maximum(jnp.maximum(best[0], best[1]), jnp.maximum(best[2], best[3]))
        total = sum(part[d] * jnp.exp(best[d] - high) for d in range(NX))
        lse = high + jnp.log(total)
        if a == 0:
            own_lse = lse
        factor = jnp.where(row < cntx[a, 0:1], jnp.exp(best[0] - lse), 0.0)
        cols = slice(a * rows, (a + 1) * rows)
        ptbuf[:, cols] = (ebuf[:, cols] * factor).astype(BF16)

    loss = jnp.sum(jnp.where(row < count, own_lse, 0.0), axis=1, keepdims=True)
    loss = loss + jnp.sum(jnp.where(valid, soft - pos, 0.0), axis=0, keepdims=True)
    lossx[0] = jnp.broadcast_to(loss, lossx.shape[1:])
    loss_x = spread(lossx, NX, xdev, ls, lr)

    def dprem(b):
        return dot(ptbuf[b * rows:(b + 1) * rows], sall[...].reshape(NX * rows, width), NN)

    def dstate(a):
        return dot(ptbuf[:, a * rows:(a + 1) * rows], pall[...].reshape(NC * rows, width), TN)

    psend[2] = dprem(3).astype(BF16)
    via_twin = send(psend.at[2], rp.at[0], ps.at[0], pr.at[0], cdev(1))
    dsend[1] = dstate(2).astype(BF16)
    via_r = send(dsend.at[1, top], r1.at[0], rs.at[0], rr.at[0], xdev(1))
    via_l = send(dsend.at[1, bot], r1.at[1], rs.at[1], rr.at[1], xdev(3))
    dsend[0] = dstate(1).astype(BF16)
    lone_r = send(dsend.at[0, bot], rx.at[0, bot], rs.at[2], rr.at[2], xdev(1))
    dsend[2] = dstate(3).astype(BF16)
    lone_l = send(dsend.at[2, top], rx.at[1, top], rs.at[3], rr.at[3], xdev(3))
    over = dprem(2)
    via_twin.wait_recv()
    psend[1] = (over + rp[0].astype(F32)).astype(BF16)
    over_p = send(psend.at[1], rp.at[2], ps.at[2], pr.at[2], cdev(2))
    psend[0] = dprem(1).astype(BF16)
    twin_p = send(psend.at[0], rp.at[1], ps.at[1], pr.at[1], cdev(1))
    via_r.wait_recv()
    dsend[0, top] = (dsend[0, top].astype(F32) + r1[0].astype(F32)).astype(BF16)
    pair_r = send(dsend.at[0, top], rx.at[0, top], rs.at[4], rr.at[4], xdev(1))
    via_l.wait_recv()
    dsend[2, bot] = (dsend[2, bot].astype(F32) + r1[1].astype(F32)).astype(BF16)
    pair_l = send(dsend.at[2, bot], rx.at[1, bot], rs.at[5], rr.at[5], xdev(3))
    own_s[...] = dstate(0)
    own_p[...] = dprem(0)

    arrive(loss_x)
    lossc[0] = lossx[0] + lossx[1] + lossx[2] + lossx[3]
    loss_c = spread_xor(lossc, ls, lr, NX)

    arrive(back_y)
    bzuf[0] = byuf[pick_y]
    back_z = spread(bzuf, NZ, zdev, ts, tr, NX + NY)

    arrive(loss_c)
    lossy[0] = lossc[0] + lossc[1] + lossc[2] + lossc[3]
    loss_y = spread(lossy, NY, ydev, ls, lr, NX + NC)

    weight = vflt + qval
    arrive([lone_r, lone_l, pair_r, pair_l])
    dstates = own_s[...] + rx[0].astype(F32) + rx[1].astype(F32)
    dstates = dstates + qval * hardb[...].astype(F32) - weight * pall[0].astype(F32)
    gsb[...] = (SCALE * dstates).astype(BF16)
    put_s = pltpu.make_async_copy(gsb, gs_hbm, local_sem.at[2])
    put_s.start()

    arrive(loss_y)
    lossz[0] = lossy[0] + lossy[1] + lossy[2] + lossy[3]
    loss_z = spread(lossz, NZ, zdev, ls, lr, NX + NC + NY)

    arrive([over_p, twin_p])
    dprems = own_p[...] + rp[1].astype(F32) + rp[2].astype(F32)
    own_p[...] = dprems - SCALE * weight * sall[0].astype(F32)

    arrive(back_z)
    home = bzuf[pick_z]
    gpb[...] = (own_p[...] + dot(place, home, NN)).astype(BF16)
    put_p = pltpu.make_async_copy(gpb, gp_hbm, local_sem.at[3])
    put_p.start()

    arrive(loss_z)
    full = lossz[0]
    for i in range(1, NZ):
        full = full + lossz[i]
    loss_ref[...] = full[0:1, 0:1] / (NX * NC * NZ * NY * rows)

    for copy in sent:
        copy.wait_send()
    put_s.wait()
    put_p.wait()


def body(states, premises, counts, partner_mask, send_rows, hard_idx):
    rows, width = states.shape
    offer = send_rows.shape[2]
    vmem = pltpu.VMEM
    dma = pltpu.SemaphoreType.DMA
    any_spec = pl.BlockSpec(memory_space=pl.ANY)
    vmem_spec = pl.BlockSpec(memory_space=pltpu.VMEM)
    smem_spec = pl.BlockSpec(memory_space=pltpu.SMEM)
    loss, gs, gp = pl.pallas_call(
        kernel,
        out_shape=(
            jax.ShapeDtypeStruct((1, 1), F32),
            jax.ShapeDtypeStruct((rows, width), BF16),
            jax.ShapeDtypeStruct((rows, width), BF16),
        ),
        in_specs=[smem_spec, smem_spec, vmem_spec, vmem_spec, any_spec, any_spec],
        out_specs=(vmem_spec, any_spec, any_spec),
        scratch_shapes=[
            vmem((NX, rows, width), BF16),
            vmem((NC, rows, width), BF16),
            vmem((NX, 8, rows), jnp.int32),
            vmem((NC, 8, rows), jnp.int32),
            vmem((NZ, offer, width), BF16),
            vmem((NY, offer, width), BF16),
            vmem((NY, offer, width), BF16),
            vmem((NZ, offer, width), BF16),
            vmem((NC * rows, NX * rows), F32),
            vmem((NC * rows, NX * rows), BF16),
            vmem((NX, 2 * NX, rows), F32),
            vmem((rows, width), BF16),
            vmem((rows, width), F32),
            vmem((rows, width), F32),
            vmem((3, rows, width), BF16),
            vmem((2, rows // 2, width), BF16),
            vmem((2, rows, width), BF16),
            vmem((3, rows, width), BF16),
            vmem((3, rows, width), BF16),
            vmem((NX, 8, 128), F32),
            vmem((NC, 8, 128), F32),
            vmem((NY, 8, 128), F32),
            vmem((NZ, 8, 128), F32),
            vmem((rows, width), BF16),
            vmem((rows, width), BF16),
            dma((4,)),
            dma((6,)), dma((6,)),
            dma((5,)), dma((5,)),
            dma((NX + NC,)), dma((NX + NC,)),
            dma((NZ + NY,)), dma((NZ + NY,)),
            dma((NX + NY + NZ,)), dma((NX + NY + NZ,)),
            dma((6,)), dma((6,)),
            dma((3,)), dma((3,)),
            dma((NX + NC + NY + NZ,)), dma((NX + NC + NY + NZ,)),
        ],
        compiler_params=pltpu.CompilerParams(collective_id=0, has_side_effects=True),
    )(
        counts,
        partner_mask,
        send_rows.reshape(1, offer),
        hard_idx.reshape(1, rows),
        states,
        premises,
    )
    return loss.reshape(()), gs, gp


def solution(mesh):
    return jax.shard_map(
        body,
        mesh=mesh,
        in_specs=(
            P(("loop", "groups"), None),
            P(("loop", "groups"), None),
            P("loop", "groups"),
            P("loop"),
            P("loop", "groups", None),
            P(("loop", "groups")),
        ),
        out_specs=(P(), P(("loop", "groups"), None), P(("loop", "groups"), None)),
        check_vma=False,
    )
```

time: 426 us -> 56.3 us (0.13)
  the two profiles are of different devices: /device:TPU:16 before, /device:TPU:8 now
where the time goes in v1:
time: 56.3 us; the launch traced here: 56.1 us
  Pallas kernels  50 us (89%)
  between operations  3.7 us (7%)
  local copies, waits for them, and re-layouts  2.42 us (4%)
    pallas_call x1, Pallas kernels, body(): pl.pallas_call(kernel, out_shape=(jax.ShapeDtypeStruct((1, 1), F32), jax....  50 us
    unnamed x4, local copies, waits for them, and re-layouts  2.42 us

profile of v1, /device:TPU:8, one launch (start us, length us, event | category | flops | bytes accessed | tf_op | source)
XLA Modules:
  0.0 56.1 jit_solution(1950461165923670180)
XLA Ops:
  1.9 50.0 %shard_map.85 = (f32[1,1]{1,0:T(1,128)}, bf16[128,1024]{1,0:T(8,128)(2,1)}, bf16[128,1024]{1,0:T(8,128)(2,1)}) custom-call(s32[1,1]{1,0:T(1,128)S(6)} %copy.12.counts_ref, s32[1]{0:T(128)S(6)} %copy.13.mask_ref, s32[1,16]{1,0:T(1,128)} %bitcast.3, s32[1,128]{1,0:T(1,128)} %bitcast.4, bf16[128,1024]{1,0:T(8,128)(2,1)} %states_hbm.1, bf16[128,1024]{1,0:T(8,128)(2,1)} %prem_hbm.1), custom_call_target="tpu_custom_call" | custom-call | tf_op jit(solution)/shard_map/pallas_call | solution.py:282
  52.6 0.0 copy-start
  52.6 1.7 %copy.15 = bf16[128,1024]{1,0:T(8,128)(2,1)} copy(bf16[128,1024]{1,0:T(8,128)(2,1)} %get-tuple-element.13) | data formatting | bytes 524288
  54.3 0.0 copy-done
  54.3 0.7 %copy.16 = bf16[128,1024]{1,0:T(8,128)(2,1)} copy(bf16[128,1024]{1,0:T(8,128)(2,1)S(1)} %copy-done) | data formatting | bytes 524288
Async XLA Ops:
  52.6 1.7 %copy-start = (bf16[128,1024]{1,0:T(8,128)(2,1)S(1)}, bf16[128,1024]{1,0:T(8,128)(2,1)}, u32[]{:S(2)}) copy-start(bf16[128,1024]{1,0:T(8,128)(2,1)} %get-tuple-element.14) | copy-start | bytes 786436

commit v2 on v1

--- a/solution.py
+++ b/solution.py
@@ -21,11 +21,12 @@
 
 
 def kernel(
-    counts_ref, mask_ref, send_ref, hidx_ref, states_hbm, prem_hbm,
-    loss_ref, gs_hbm, gp_hbm,
+    counts_ref, mask_ref, send_hbm, hidx_hbm, states_hbm, prem_hbm,
+    loss_ref, gs_ref, gp_ref,
+    send_ref, hidx_ref,
     sall, pall, cntx, cnty, zbuf, ybuf, byuf, bzuf,
     ebuf, ptbuf, stats, hardb, own_s, own_p,
-    dsend, r1, rx, psend, rp, lossx, lossc, lossy, lossz, gsb, gpb,
+    dsend, r1, rx, psend, rp, lossg, lossy, lossz,
     local_sem, xs, xr, ys, yr, cs, cr, zs, zr, ts, tr, rs, rr, ps, pr, ls, lr,
 ):
     rows, width = states_hbm.shape
@@ -46,6 +47,12 @@
         c = (c + flip % 2) % 2
         return {"loop": x * NC + y * 2 + c, "groups": g}
 
+    def gdev(step, flip):
+        y, c = yc // 2, yc % 2
+        y = (y + flip // 2) % 2
+        c = (c + flip % 2) % 2
+        return {"loop": ((x + step) % NX) * NC + y * 2 + c, "groups": g}
+
     def zdev(step):
         return {"loop": me, "groups": yh * NZ + (z + step) % NZ}
 
@@ -64,9 +71,10 @@
         return copy
 
     def spread(buf, n, devs, ssem, rsem, base=0):
+        order = sorted(range(1, n), key=lambda i: -min(i, n - i))
         return [
             send(buf.at[0], buf.at[n - i], ssem.at[base + i], rsem.at[base + n - i], devs(i))
-            for i in range(1, n)
+            for i in order
         ]
 
     def spread_xor(buf, ssem, rsem, base=0):
@@ -79,26 +87,31 @@
         for copy in copies:
             copy.wait_recv()
 
-    load_p = pltpu.make_async_copy(prem_hbm, pall.at[0], local_sem.at[0])
-    load_s = pltpu.make_async_copy(states_hbm, sall.at[0], local_sem.at[1])
-    load_p.start()
-    load_s.start()
-
     barrier = pltpu.get_barrier_semaphore()
-    peers = [xdev(i) for i in range(1, NX)] + [cdev(i) for i in range(1, NC)]
-    peers += [zdev(i) for i in range(1, NZ)] + [ydev(i) for i in range(1, NY)]
+    mates = [(i, j) for i in range(NX) for j in range(NC) if i or j]
+    peers = [zdev(i) for i in (4, 3, 5, 2, 6, 1, 7)] + [ydev(i) for i in (2, 1, 3)]
+    peers += [gdev(i, j) for i, j in mates]
     for peer in peers:
         pl.semaphore_signal(barrier, inc=1, device_id=peer, device_id_type=pl.DeviceIdType.MESH)
+    pairs = [
+        (prem_hbm, pall.at[0]), (send_hbm, send_ref), (states_hbm, sall.at[0]),
+        (hidx_hbm, hidx_ref),
+    ]
+    loads = [pltpu.make_async_copy(a, b, local_sem.at[i]) for i, (a, b) in enumerate(pairs)]
+    for load in loads:
+        load.start()
+    loads[0].wait()
+    loads[1].wait()
+    place = lax.broadcasted_iota(jnp.int32, (rows, offer), 0) == send_ref[...]
+    place = place.astype(F32).astype(BF16)
+    zbuf[0] = dot(place, pall[0], TN).astype(BF16)
+    for load in loads[2:]:
+        load.wait()
 
     count = counts_ref[0, 0]
     mask = mask_ref[0]
     cntx[0] = jnp.full(cntx.shape[1:], count, jnp.int32)
     cnty[0] = jnp.full(cnty.shape[1:], count, jnp.int32)
-    place = lax.broadcasted_iota(jnp.int32, (rows, offer), 0) == send_ref[...]
-    place = place.astype(F32).astype(BF16)
-    load_p.wait()
-    zbuf[0] = dot(place, pall[0], TN).astype(BF16)
-    load_s.wait()
     pl.semaphore_wait(barrier, len(peers))
 
     offers_z = spread(zbuf, NZ, zdev, zs, zr)
@@ -192,8 +205,11 @@
 
     loss = jnp.sum(jnp.where(row < count, own_lse, 0.0), axis=1, keepdims=True)
     loss = loss + jnp.sum(jnp.where(valid, soft - pos, 0.0), axis=0, keepdims=True)
-    lossx[0] = jnp.broadcast_to(loss, lossx.shape[1:])
-    loss_x = spread(lossx, NX, xdev, ls, lr)
+    lossg[0] = jnp.broadcast_to(loss, lossg.shape[1:])
+    loss_g = []
+    for i, j in mates:
+        to, here = i * NC + j, (NX - i) % NX * NC + j
+        loss_g.append(send(lossg.at[0], lossg.at[here], ls.at[to], lr.at[here], gdev(i, j)))
 
     def dprem(b):
         return dot(ptbuf[b * rows:(b + 1) * rows], sall[...].reshape(NX * rows, width), NN)
@@ -216,57 +232,61 @@
     over_p = send(psend.at[1], rp.at[2], ps.at[2], pr.at[2], cdev(2))
     psend[0] = dprem(1).astype(BF16)
     twin_p = send(psend.at[0], rp.at[1], ps.at[1], pr.at[1], cdev(1))
+    own_s[...] = dstate(0)
+    own_p[...] = dprem(0)
+    weight = vflt + qval
+    own_s[...] += qval * hardb[...].astype(F32) - weight * pall[0].astype(F32)
+    own_p[...] -= SCALE * weight * sall[0].astype(F32)
+
+    arrive(back_y)
+    bzuf[0] = byuf[pick_y]
+    back_z = spread(bzuf, NZ, zdev, ts, tr, NX + NY)
+
+    def total(buf):
+        value = buf[0]
+        for i in range(1, buf.shape[0]):
+            value = value + buf[i]
+        return value
+
+    arrive(loss_g)
+    lossy[0] = total(lossg)
+    loss_y = spread(lossy, NY, ydev, ls, lr, NX * NC)
+
     via_r.wait_recv()
     dsend[0, top] = (dsend[0, top].astype(F32) + r1[0].astype(F32)).astype(BF16)
     pair_r = send(dsend.at[0, top], rx.at[0, top], rs.at[4], rr.at[4], xdev(1))
     via_l.wait_recv()
     dsend[2, bot] = (dsend[2, bot].astype(F32) + r1[1].astype(F32)).astype(BF16)
     pair_l = send(dsend.at[2, bot], rx.at[1, bot], rs.at[5], rr.at[5], xdev(3))
-    own_s[...] = dstate(0)
-    own_p[...] = dprem(0)
-
-    arrive(loss_x)
-    lossc[0] = lossx[0] + lossx[1] + lossx[2] + lossx[3]
-    loss_c = spread_xor(lossc, ls, lr, NX)
-
-    arrive(back_y)
-    bzuf[0] = byuf[pick_y]
-    back_z = spread(bzuf, NZ, zdev, ts, tr, NX + NY)
-
-    arrive(loss_c)
-    lossy[0] = lossc[0] + lossc[1] + lossc[2] + lossc[3]
-    loss_y = spread(lossy, NY, ydev, ls, lr, NX + NC)
-
-    weight = vflt + qval
+
+    arrive(loss_y)
+    lossz[0] = total(lossy)
+    loss_z = spread(lossz, NZ, zdev, ls, lr, NX * NC + NY)
+
+    arrive([over_p, twin_p])
+    own_p[...] += rp[1].astype(F32) + rp[2].astype(F32)
+
     arrive([lone_r, lone_l, pair_r, pair_l])
     dstates = own_s[...] + rx[0].astype(F32) + rx[1].astype(F32)
-    dstates = dstates + qval * hardb[...].astype(F32) - weight * pall[0].astype(F32)
-    gsb[...] = (SCALE * dstates).astype(BF16)
-    put_s = pltpu.make_async_copy(gsb, gs_hbm, local_sem.at[2])
-    put_s.start()
-
-    arrive(loss_y)
-    lossz[0] = lossy[0] + lossy[1] + lossy[2] + lossy[3]
-    loss_z = spread(lossz, NZ, zdev, ls, lr, NX + NC + NY)
-
-    arrive([over_p, twin_p])
-    dprems = own_p[...] + rp[1].astype(F32) + rp[2].astype(F32)
-    own_p[...] = dprems - SCALE * weight * sall[0].astype(F32)
+    gs_ref[...] = (SCALE * dstates).astype(BF16)
 
     arrive(back_z)
     home = bzuf[pick_z]
-    gpb[...] = (own_p[...] + dot(place, home, NN)).astype(BF16)
-    put_p = pltpu.make_async_copy(gpb, gp_hbm, local_sem.at[3])
-    put_p.start()
+    gp_ref[...] = (own_p[...] + dot(place, home, NN)).astype(BF16)
 
     arrive(loss_z)
-    full = lossz[0]
-    for i in range(1, NZ):
-        full = full + lossz[i]
-    loss_ref[...] = full[0:1, 0:1] / (NX * NC * NZ * NY * rows)
+    loss_ref[...] = total(lossz) / (NX * NC * NZ * NY * rows)
 
     for copy in sent:
         copy.wait_send()
+
+
+def flush(loss_ref, gs_ref, gp_ref, loss_out, gs_out, gp_out, sem):
+    put_s = pltpu.make_async_copy(gs_ref, gs_out, sem.at[0])
+    put_p = pltpu.make_async_copy(gp_ref, gp_out, sem.at[1])
+    put_s.start()
+    put_p.start()
+    loss_out[...] = loss_ref[0:1, 0:1]
     put_s.wait()
     put_p.wait()
 
@@ -281,14 +301,12 @@
     smem_spec = pl.BlockSpec(memory_space=pltpu.SMEM)
     loss, gs, gp = pl.pallas_call(
         kernel,
-        out_shape=(
-            jax.ShapeDtypeStruct((1, 1), F32),
-            jax.ShapeDtypeStruct((rows, width), BF16),
-            jax.ShapeDtypeStruct((rows, width), BF16),
-        ),
-        in_specs=[smem_spec, smem_spec, vmem_spec, vmem_spec, any_spec, any_spec],
-        out_specs=(vmem_spec, any_spec, any_spec),
+        out_shape=(vmem((8, 128), F32), vmem((rows, width), BF16), vmem((rows, width), BF16)),
+        in_specs=[smem_spec] * 2 + [any_spec] * 4,
+        out_specs=(vmem_spec,) * 3,
         scratch_shapes=[
+            vmem((1, offer), jnp.int32),
+            vmem((1, rows), jnp.int32),
             vmem((NX, rows, width), BF16),
             vmem((NC, rows, width), BF16),
             vmem((NX, 8, rows), jnp.int32),
@@ -308,12 +326,9 @@
             vmem((2, rows, width), BF16),
             vmem((3, rows, width), BF16),
             vmem((3, rows, width), BF16),
-            vmem((NX, 8, 128), F32),
-            vmem((NC, 8, 128), F32),
+            vmem((NX * NC, 8, 128), F32),
             vmem((NY, 8, 128), F32),
             vmem((NZ, 8, 128), F32),
-            vmem((rows, width), BF16),
-            vmem((rows, width), BF16),
             dma((4,)),
             dma((6,)), dma((6,)),
             dma((5,)), dma((5,)),
@@ -322,7 +337,7 @@
             dma((NX + NY + NZ,)), dma((NX + NY + NZ,)),
             dma((6,)), dma((6,)),
             dma((3,)), dma((3,)),
-            dma((NX + NC + NY + NZ,)), dma((NX + NC + NY + NZ,)),
+            dma((NX * NC + NY + NZ,)), dma((NX * NC + NY + NZ,)),
         ],
         compiler_params=pltpu.CompilerParams(collective_id=0, has_side_effects=True),
     )(
@@ -333,6 +348,18 @@
         states,
         premises,
     )
+    loss, gs, gp = pl.pallas_call(
+        flush,
+        out_shape=(
+            jax.ShapeDtypeStruct((1, 1), F32),
+            jax.ShapeDtypeStruct((rows, width), BF16),
+            jax.ShapeDtypeStruct((rows, width), BF16),
+        ),
+        in_specs=[vmem_spec, any_spec, any_spec],
+        out_specs=(vmem_spec, any_spec, any_spec),
+        scratch_shapes=[dma((2,))],
+        compiler_params=pltpu.CompilerParams(vmem_limit_bytes=2**20),
+    )(loss, gs, gp)
     return loss.reshape(()), gs, gp
 
 

time: 56.3 us -> 50 us (0.89)
  the two profiles are of different devices: /device:TPU:8 before, /device:TPU:1 now
where the time goes in v2:
time: 50 us; the launch traced here: 49.9 us
  Pallas kernels  48 us (96%)
  between operations  1.93 us (4%)
    pallas_call x1, Pallas kernels, body(): pl.pallas_call(kernel, out_shape=(vmem((8, 128), F32), vmem((rows, width)...  46.6 us
    pallas_call x1, Pallas kernels, body(): pl.pallas_call(flush, out_shape=(jax.ShapeDtypeStruct((1, 1), F32), jax.S...  1.32 us

profile of v2, /device:TPU:1, one launch (start us, length us, event | category | flops | bytes accessed | tf_op | source)
XLA Modules:
  0.0 49.9 jit_solution(12610464484805320873)
XLA Ops:
  1.9 46.6 %shard_map.85 = (f32[8,128]{1,0:T(8,128)S(1)}, bf16[128,1024]{1,0:T(8,128)(2,1)S(1)}, bf16[128,1024]{1,0:T(8,128)(2,1)S(1)}) custom-call(s32[1,1]{1,0:T(1,128)S(6)} %copy.9.counts_ref, s32[1]{0:T(128)S(6)} %copy.10.mask_ref, s32[1,16]{1,0:T(1,128)} %bitcast.3, s32[1,128]{1,0:T(1,128)} %bitcast.4, bf16[128,1024]{1,0:T(8,128)(2,1)} %states_hbm.1, ...), custom_call_target="tpu_custom_call" | custom-call | tf_op jit(solution)/shard_map/pallas_call | solution.py:302
  48.6 1.3 %shard_map.86 = (f32[1,1]{1,0:T(1,128)}, bf16[128,1024]{1,0:T(8,128)(2,1)}, bf16[128,1024]{1,0:T(8,128)(2,1)}) custom-call(f32[8,128]{1,0:T(8,128)S(1)} %get-tuple-element.9.loss_ref, bf16[128,1024]{1,0:T(8,128)(2,1)S(1)} %get-tuple-element.10.gs_ref, bf16[128,1024]{1,0:T(8,128)(2,1)S(1)} %get-tuple-element.11.gp_ref), custom_call_target="tpu_custom_call" | custom-call | tf_op jit(solution)/shard_map/pallas_call | solution.py:351
